TPU v7x, 512 devices: a whole 4x8x8 slice. The times are simulated.
512 devices in a mesh: layer: 2 (over core), row: 16 (over x, z_hi), col: 16 (over z_lo, y).
Axes of the slice: x: 4, y: 8, z: 8 (z_hi: 4, z_lo: 2; z = z_hi * 2 + z_lo), core: 2. Of those that a mesh axis runs over, the one named last changes fastest.
Arguments:
- rhs_sub: float32 [2, 3, 1, 16, 256, 512], P('layer', None, None, 'row', 'col'), may hold values from -6 to 6
- rhs_top: float32 [1, 16, 256, 512], P(None, 'row', 'col'), may hold values from -6 to 6
- lower_inv_sub: float32 [2, 3, 1, 16, 256, 256], P('layer', None, None, 'row', 'col'), as said below
- lower_inv_top: float32 [1, 16, 256, 256], P(None, 'row', 'col'), as said below
- upper_inv_sub: float32 [2, 3, 1, 16, 256, 256], P('layer', None, None, 'row', 'col'), as said below
- upper_inv_top: float32 [1, 16, 256, 256], P(None, 'row', 'col'), as said below
- lower_sub: float32 [2, 3, 1, 16, 1, 16, 256, 256], P('layer', None, None, 'row', None, 'col'), may hold values from -0.09375 to 0.09375
- lower_top: float32 [2, 3, 1, 16, 1, 16, 256, 256], P('layer', None, None, 'row', None, 'col'), may hold values from -0.0546875 to 0.0546875
- upper_sub: float32 [2, 3, 1, 16, 1, 16, 256, 256], P('layer', None, None, 'row', None, 'col'), may hold values from -0.0625 to 0.0625
- upper_top: float32 [2, 3, 1, 16, 1, 16, 256, 256], P('layer', None, None, 'row', None, 'col'), may hold values from -0.09375 to 0.09375
- block_pattern: int32 [2, 4, 3, 1, 16, 1, 16], P('layer', None, None, None, 'row', None, 'col'), may hold values 0 or 1
Outputs:
- solution_sub: float32 [2, 3, 1, 16, 256, 512], P('layer', None, None, 'row', 'col')
- solution_top: float32 [1, 16, 256, 512], P(None, 'row', 'col')
Inputs may be any that keep to these rules, and one draw needn't show every extreme that they name: `lower_inv_sub`: every 256 x 256 block is lower triangular with unit diagonal. `lower_inv_top`: every 256 x 256 block is lower triangular with unit diagonal. `upper_inv_sub`: every 256 x 256 block is upper triangular with unit diagonal. `upper_inv_top`: every 256 x 256 block is upper triangular with unit diagonal.
All inputs are finite; a program needn't handle non-finite values. No bound on the sum of `block_pattern` on one device may be relied on, other than what follows from the above.
Results may differ from a plain program's by a relative error of at most 0.00014.
Values sent between devices are 32-bit elements; how exact they have to be, the bound alone decides.
No kernel may reach another device: no remote copies, remote signals or barrier semaphores. Data moves between devices by JAX's collectives and lax.ppermute only.
A program may use at most 64 MiB of HBM per device.

v0:
```python
import jax
import jax.numpy as jnp
from jax import lax
from jax.sharding import PartitionSpec as P

HIGHEST = lax.Precision.HIGHEST


def broadcast(x, axis, root):
    mine = lax.axis_index(axis) == root
    return lax.psum(jnp.where(mine, x, jnp.zeros_like(x)), axis)


def couple(blocks, pattern, solution):
    weighted = solution[None] * pattern[:, :, None, None].astype(jnp.float32)
    return jnp.einsum("tsab,tsbn->tan", blocks, weighted, precision=HIGHEST)


def spread(whole_block):
    return broadcast(whole_block, "row", lax.axis_index("col"))


def on_device(
    rhs_sub,
    rhs_top,
    lower_inv_sub,
    lower_inv_top,
    upper_inv_sub,
    upper_inv_top,
    lower_sub,
    lower_top,
    upper_sub,
    upper_top,
    block_pattern,
):
    lower_list = [lower_inv_sub[0, level, :, 0] for level in range(3)] + [lower_inv_top[:, 0]]
    upper_list = [upper_inv_sub[0, level, :, 0] for level in range(3)] + [upper_inv_top[:, 0]]
    right_sides = [rhs_sub[0, level, :, 0] for level in range(3)] + [rhs_top[:, 0]]

    def solve(partial_value, right_side, inverse_rows, top):
        if partial_value is None:
            residual = right_side
        else:
            share = lax.psum_scatter(partial_value, "col", scatter_dimension=1, tiled=True)
            if top:
                share = lax.psum(share, "layer")
            residual = right_side - share
        return jnp.einsum(
            "kab,kbn->kan",
            inverse_rows,
            lax.all_gather(residual, "col", axis=1, tiled=True),
            precision=HIGHEST,
        )

    def copy_out(solution):
        return spread(lax.all_gather(solution, "col", axis=1, tiled=True))

    def blocks(array, pair):
        return array[0, pair, :, 0, :, 0]

    def pattern(kind, pair):
        return block_pattern[0, kind, pair, :, 0, :, 0]

    fore_zero = solve(None, right_sides[0], lower_list[0], False)
    copy_zero = copy_out(fore_zero)
    into_one = couple(blocks(lower_sub, 0), pattern(0, 0), copy_zero)
    into_two = couple(blocks(lower_sub, 1), pattern(0, 1), copy_zero)
    into_top = couple(blocks(lower_top, 0), pattern(1, 0), copy_zero)
    fore_one = solve(into_one, right_sides[1], lower_list[1], False)
    copy_one = copy_out(fore_one)
    into_two = into_two + couple(blocks(lower_sub, 2), pattern(0, 2), copy_one)
    into_top = into_top + couple(blocks(lower_top, 1), pattern(1, 1), copy_one)
    fore_two = solve(into_two, right_sides[2], lower_list[2], False)
    copy_two = copy_out(fore_two)
    into_top = into_top + couple(blocks(lower_top, 2), pattern(1, 2), copy_two)
    fore_top = solve(into_top, right_sides[3], lower_list[3], True)
    final_top = solve(None, fore_top, upper_list[3], False)
    down_top = copy_out(final_top)
    toward_two = couple(blocks(upper_top, 2), pattern(3, 2), down_top)
    toward_one = couple(blocks(upper_top, 1), pattern(3, 1), down_top)
    toward_zero = couple(blocks(upper_top, 0), pattern(3, 0), down_top)
    final_two = solve(toward_two, fore_two, upper_list[2], False)
    down_two = copy_out(final_two)
    toward_one = toward_one + couple(blocks(upper_sub, 2), pattern(2, 2), down_two)
    toward_zero = toward_zero + couple(blocks(upper_sub, 1), pattern(2, 1), down_two)
    final_one = solve(toward_one, fore_one, upper_list[1], False)
    down_one = copy_out(final_one)
    toward_zero = toward_zero + couple(blocks(upper_sub, 0), pattern(2, 0), down_one)
    final_zero = solve(toward_zero, fore_zero, upper_list[0], False)
    solution_sub = jnp.stack([final_zero, final_one, final_two])[None, :, :, None]
    solution_top = final_top[:, None]
    return (solution_sub, solution_top)


def solution(mesh):
    placed = (
        P("layer", None, None, "row", "col", None),
        P(None, "row", "col", None),
        P("layer", None, None, "row", "col", None),
        P(None, "row", "col", None),
        P("layer", None, None, "row", "col", None),
        P(None, "row", "col", None),
        P("layer", None, None, "row", None, "col", None, None),
        P("layer", None, None, "row", None, "col", None, None),
        P("layer", None, None, "row", None, "col", None, None),
        P("layer", None, None, "row", None, "col", None, None),
        P("layer", None, None, None, "row", None, "col"),
    )
    return jax.shard_map(
        on_device,
        mesh=mesh,
        in_specs=placed,
        out_specs=(P("layer", None, None, "row", "col", None), P(None, "row", "col", None)),
        check_vma=False,
    )
```

profile of v0, /device:TPU:2, one launch (start us, length us, event | category | flops | bytes accessed | tf_op | source)
XLA Modules:
  0.0 2184.0 jit_solution(2908091870607377560)
XLA Ops:
  8.0 37.7 %all-gather = f32[1,1,1,1,256,512]{5,4,3,2,1,0:T(8,128)S(1)} all-gather(f32[1,1,1,1,16,512]{5,4,3,2,1,0:T(8,128)S(1)} %get-tuple-element.8), channel_id=2, replica_groups=mesh['layer'=2,'row'=16,'col'=16] {'col'}, dimensions={4}, use_global_device_ids=true | all-gather | bytes 557056 | tf_op jit(solution)/shard_map/all_gather | solution.py:51
  46.1 32.3 %all-gather.1 = f32[256,512]{1,0:T(8,128)S(1)} all-gather(f32[16,512]{1,0:T(8,128)S(1)} %fusion.33), channel_id=3, replica_groups=mesh['layer'=2,'row'=16,'col'=16] {'col'}, dimensions={0}, use_global_device_ids=true | all-gather | bytes 557056 | tf_op jit(solution)/shard_map/all_gather | solution.py:56
  78.4 0.8 select_bitcast_fusion.5
  81.3 168.6 %all-reduce.13.cloned.1.call-done = f32[1,256,512]{2,1,0:T(8,128)} async-done(((f32[1,256,512]{2,1,0:T(8,128)}), f32[1,256,512]{2,1,0:T(8,128)}) %all-reduce.13.cloned.1.call-update) | async-done | bytes 524304 | tf_op jit(solution)/shard_map/psum | solution.py:11
  249.9 2.0 convolution_bitcast_fusion.1
  252.0 1.0 copy.24
  253.1 1.3 dynamic-slice
  255.0 140.9 %all-reduce.25.cloned.1.call-done = f32[1,256,512]{2,0,1:T(1,128)} async-done(((f32[1,256,512]{2,0,1:T(1,128)}), f32[1,256,512]{2,0,1:T(1,128)}) %all-reduce.25.cloned.1.call-update) | async-done | bytes 524304
  395.9 0.8 fusion.84
  396.7 35.3 %all_gather.44 = f32[1,256,512]{2,0,1:T(1,128)S(1)} all-gather(f32[1,16,512]{2,0,1:T(1,128)S(1)} %fusion.84), channel_id=1, replica_groups=mesh['layer'=2,'row'=16,'col'=16] {'col'}, dimensions={1}, use_global_device_ids=true | all-gather | bytes 557056 | tf_op jit(solution)/shard_map/all_gather | solution.py:51
  432.4 32.3 %all-gather.2 = f32[256,512]{1,0:T(8,128)S(1)} all-gather(f32[16,512]{1,0:T(8,128)S(1)} %bitcast.205), channel_id=4, replica_groups=mesh['layer'=2,'row'=16,'col'=16] {'col'}, dimensions={0}, use_global_device_ids=true | all-gather | bytes 557056 | tf_op jit(solution)/shard_map/all_gather | solution.py:56
  464.7 0.9 select_bitcast_fusion.4
  467.0 1.0 fusion.27
  468.0 165.1 %all-reduce.15.cloned.1.call-done = f32[1,256,512]{2,1,0:T(8,128)} async-done(((f32[1,256,512]{2,1,0:T(8,128)}), f32[1,256,512]{2,1,0:T(8,128)}) %all-reduce.15.cloned.1.call-update) | async-done | bytes 524304 | tf_op jit(solution)/shard_map/psum | solution.py:11
  633.1 2.0 fusion.3
  635.2 1.0 copy.26
  638.1 141.0 %all-reduce.27.cloned.1.call-done = f32[1,256,512]{2,0,1:T(1,128)} async-done(((f32[1,256,512]{2,0,1:T(1,128)}), f32[1,256,512]{2,0,1:T(1,128)}) %all-reduce.27.cloned.1.call-update) | async-done | bytes 524304
  779.1 0.8 fusion.83
  779.9 35.3 %all_gather.46 = f32[1,256,512]{2,0,1:T(1,128)S(1)} all-gather(f32[1,16,512]{2,0,1:T(1,128)S(1)} %fusion.83), channel_id=1, replica_groups=mesh['layer'=2,'row'=16,'col'=16] {'col'}, dimensions={1}, use_global_device_ids=true | all-gather | bytes 557056 | tf_op jit(solution)/shard_map/all_gather | solution.py:51
  815.6 32.3 %all-gather.3 = f32[256,512]{1,0:T(8,128)S(1)} all-gather(f32[16,512]{1,0:T(8,128)S(1)} %bitcast.206), channel_id=5, replica_groups=mesh['layer'=2,'row'=16,'col'=16] {'col'}, dimensions={0}, use_global_device_ids=true | all-gather | bytes 557056 | tf_op jit(solution)/shard_map/all_gather | solution.py:56
  847.9 0.9 select_bitcast_fusion.3
  849.3 1.0 fusion.31
  850.3 1.0 convolution_add_fusion.5
  851.3 165.0 %all-reduce.17.cloned.1.call-done = f32[1,256,512]{2,1,0:T(8,128)} async-done(((f32[1,256,512]{2,1,0:T(8,128)}), f32[1,256,512]{2,1,0:T(8,128)}) %all-reduce.17.cloned.1.call-update) | async-done | bytes 524304 | tf_op jit(solution)/shard_map/psum | solution.py:11
  1016.3 2.0 fusion.2
  1018.3 1.1 copy.27
  1019.5 142.8 %all-reduce.29.cloned.1.call-done = f32[1,256,512]{2,0,1:T(1,128)} async-done(((f32[1,256,512]{2,0,1:T(1,128)}), f32[1,256,512]{2,0,1:T(1,128)}) %all-reduce.29.cloned.1.call-update) | async-done | bytes 524304
  1163.1 3.5 psum.52
  1166.7 35.3 %all_gather.48 = f32[1,256,512]{2,0,1:T(1,128)S(1)} all-gather(f32[1,16,512]{2,0,1:T(1,128)S(1)} %reshape_subtract_fusion), channel_id=1, replica_groups=mesh['layer'=2,'row'=16,'col'=16] {'col'}, dimensions={1}, use_global_device_ids=true | all-gather | bytes 557056 | tf_op jit(solution)/shard_map/all_gather | solution.py:51
  1202.3 32.8 %all-gather.4 = f32[256,512]{1,0:T(8,128)S(1)} all-gather(f32[16,512]{1,0:T(8,128)S(1)} %convolution_bitcast_fusion.3), channel_id=6, replica_groups=mesh['layer'=2,'row'=16,'col'=16] {'col'}, dimensions={0}, use_global_device_ids=true | all-gather | bytes 557056 | tf_op jit(solution)/shard_map/all_gather | solution.py:51
  1235.5 34.6 %all-gather.5 = f32[256,512]{1,0:T(8,128)S(1)} all-gather(f32[16,512]{1,0:T(8,128)S(1)} %bitcast.211), channel_id=7, replica_groups=mesh['layer'=2,'row'=16,'col'=16] {'col'}, dimensions={0}, use_global_device_ids=true | all-gather | bytes 557056 | tf_op jit(solution)/shard_map/all_gather | solution.py:56
  1270.0 0.8 select_bitcast_fusion.2
  1271.6 165.4 %all-reduce.19.cloned.1.call-done = f32[1,256,512]{2,1,0:T(8,128)} async-done(((f32[1,256,512]{2,1,0:T(8,128)}), f32[1,256,512]{2,1,0:T(8,128)}) %all-reduce.19.cloned.1.call-update) | async-done | bytes 524304 | tf_op jit(solution)/shard_map/psum | solution.py:11
  1437.0 2.5 convolution_bitcast_fusion
  1439.5 75.0 %reduce-scatter.4.cloned.1.call-done = f32[1,16,512]{2,1,0:T(8,128)} async-done(((f32[1,256,512]{2,1,0:T(8,128)}), f32[1,16,512]{2,1,0:T(8,128)}) %reduce-scatter.4.cloned.1.call-update) | async-done | bytes 32784 | tf_op jit(solution)/shard_map/reduce_scatter | solution.py:44
  1515.3 33.9 %all_gather.51 = f32[1,256,512]{2,1,0:T(8,128)S(1)} all-gather(f32[1,16,512]{2,1,0:T(8,128)S(1)} %bitcast_subtract_fusion.1), channel_id=1, replica_groups=mesh['layer'=2,'row'=16,'col'=16] {'col'}, dimensions={1}, use_global_device_ids=true | all-gather | bytes 557056 | tf_op jit(solution)/shard_map/all_gather | solution.py:51
  1549.6 33.3 %all-gather.6 = f32[256,512]{1,0:T(8,128)S(1)} all-gather(f32[16,512]{1,0:T(8,128)S(1)} %bitcast.207), channel_id=8, replica_groups=mesh['layer'=2,'row'=16,'col'=16] {'col'}, dimensions={0}, use_global_device_ids=true | all-gather | bytes 557056 | tf_op jit(solution)/shard_map/all_gather | solution.py:56
  1582.9 0.9 select_bitcast_fusion.1
  1586.2 164.1 %all-reduce.21.cloned.1.call-done = f32[1,256,512]{2,1,0:T(8,128)} async-done(((f32[1,256,512]{2,1,0:T(8,128)}), f32[1,256,512]{2,1,0:T(8,128)}) %all-reduce.21.cloned.1.call-update) | async-done | bytes 524304 | tf_op jit(solution)/shard_map/psum | solution.py:11
  1750.4 2.5 fusion.1
  1754.8 73.1 %reduce-scatter.6.cloned.1.call-done = f32[1,16,512]{2,1,0:T(8,128)} async-done(((f32[1,256,512]{2,1,0:T(8,128)}), f32[1,16,512]{2,1,0:T(8,128)}) %reduce-scatter.6.cloned.1.call-update) | async-done | bytes 32784 | tf_op jit(solution)/shard_map/reduce_scatter | solution.py:44
  1828.6 33.8 %all_gather.53 = f32[1,256,512]{2,1,0:T(8,128)S(1)} all-gather(f32[1,16,512]{2,1,0:T(8,128)S(1)} %bitcast_subtract_fusion), channel_id=1, replica_groups=mesh['layer'=2,'row'=16,'col'=16] {'col'}, dimensions={1}, use_global_device_ids=true | all-gather | bytes 557056 | tf_op jit(solution)/shard_map/all_gather | solution.py:51
  1862.8 33.3 %all-gather.7 = f32[256,512]{1,0:T(8,128)S(1)} all-gather(f32[16,512]{1,0:T(8,128)S(1)} %bitcast.209), channel_id=9, replica_groups=mesh['layer'=2,'row'=16,'col'=16] {'col'}, dimensions={0}, use_global_device_ids=true | all-gather | bytes 557056 | tf_op jit(solution)/shard_map/all_gather | solution.py:56
  1896.1 0.9 select_bitcast_fusion
  1898.8 165.3 %all-reduce.23.cloned.1.call-done = f32[1,256,512]{2,1,0:T(8,128)} async-done(((f32[1,256,512]{2,1,0:T(8,128)}), f32[1,256,512]{2,1,0:T(8,128)}) %all-reduce.23.cloned.1.call-update) | async-done | bytes 524304 | tf_op jit(solution)/shard_map/psum | solution.py:11
  2064.1 2.5 fusion
  2066.6 75.0 %reduce-scatter.8.cloned.1.call-done = f32[1,16,512]{2,1,0:T(8,128)} async-done(((f32[1,256,512]{2,1,0:T(8,128)}), f32[1,16,512]{2,1,0:T(8,128)}) %reduce-scatter.8.cloned.1.call-update) | async-done | bytes 32784 | tf_op jit(solution)/shard_map/reduce_scatter | solution.py:44
  2142.4 33.8 %all_gather.55 = f32[1,256,512]{2,1,0:T(8,128)S(1)} all-gather(f32[1,16,512]{2,1,0:T(8,128)S(1)} %bitcast_subtract_fusion.2), channel_id=1, replica_groups=mesh['layer'=2,'row'=16,'col'=16] {'col'}, dimensions={1}, use_global_device_ids=true | all-gather | bytes 557056 | tf_op jit(solution)/shard_map/all_gather | solution.py:51
  (73 shorter events, 12.6 us)
Async XLA Ops:
  7.2 1194.8 %copy-start = (f32[1,1,16,256]{3,2,1,0:T(8,128)S(1)}, f32[1,1,16,256]{3,2,1,0:T(8,128)}, u32[]{:S(2)}) copy-start(f32[1,1,16,256]{3,2,1,0:T(8,128)} %param.14) | copy-start | bytes 49156
  7.2 242.7 %all-reduce.13.cloned.1.call-start = ((), (), s32[]{:S(2)}) async-start(), calls=%async_computation.3 | async-start | bytes 1048576 | tf_op jit(solution)/shard_map/psum | solution.py:11
  8.0 37.7 %copy-start.10 = (f32[1,3,1,1,16,256]{5,4,3,2,1,0:T(8,128)S(1)}, f32[1,3,1,1,16,256]{5,4,3,2,1,0:T(8,128)}, u32[]{:S(2)}) copy-start(f32[1,3,1,1,16,256]{5,4,3,2,1,0:T(8,128)} %param.13) | copy-start | bytes 147460
  78.4 171.5 %copy-start.6 = (f32[1,3,1,1,1,1,256,256]{7,6,5,4,3,2,1,0:T(8,128)S(1)}, f32[1,3,1,1,1,1,256,256]{7,6,5,4,3,2,1,0:T(8,128)}, u32[]{:S(2)}) copy-start(f32[1,3,1,1,1,1,256,256]{7,6,5,4,3,2,1,0:T(8,128)} %param.17) | copy-start | bytes 2359300
  79.3 0.7 copy-start.13
  79.3 316.6 %all-reduce.25.cloned.1.call-start = ((), (), s32[]{:S(2)}) async-start(), calls=%async_computation.12 | async-start | bytes 1048576
  253.0 380.1 %all-reduce.15.cloned.1.call-start = ((), (), s32[]{:S(2)}) async-start(), calls=%async_computation.4 | async-start | bytes 1048576 | tf_op jit(solution)/shard_map/psum | solution.py:11
  465.6 1.4 copy-start.1
  465.6 313.5 %all-reduce.27.cloned.1.call-start = ((), (), s32[]{:S(2)}) async-start(), calls=%async_computation.13 | async-start | bytes 1048576
  636.2 380.1 %all-reduce.17.cloned.1.call-start = ((), (), s32[]{:S(2)}) async-start(), calls=%async_computation.5 | async-start | bytes 1048576 | tf_op jit(solution)/shard_map/psum | solution.py:11
  847.9 1.3 copy-start.7
  848.8 313.5 %all-reduce.29.cloned.1.call-start = ((), (), s32[]{:S(2)}) async-start(), calls=%async_computation.14 | async-start | bytes 1048576
  849.3 1.0 copy-start.3
  1019.4 417.5 %all-reduce.19.cloned.1.call-start = ((), (), s32[]{:S(2)}) async-start(), calls=%async_computation.6 | async-start | bytes 1048576 | tf_op jit(solution)/shard_map/psum | solution.py:11
  1163.1 3.5 copy-start.12
  1202.3 32.8 %copy-start.14 = (f32[1,1,16,256]{3,2,1,0:T(8,128)S(1)}, f32[1,1,16,256]{3,2,1,0:T(8,128)}, u32[]{:S(2)}) copy-start(f32[1,1,16,256]{3,2,1,0:T(8,128)} %param.16) | copy-start | bytes 49156
  1235.5 34.6 %copy-start.9 = (f32[512,16]{0,1:T(8,128)}, f32[512,16]{0,1:T(8,128)S(1)}, u32[]{:S(2)}) copy-start(f32[512,16]{0,1:T(8,128)S(1)} %fusion.88) | copy-start | bytes 98308
  1270.0 166.9 %copy-start.5 = (f32[1,3,1,1,1,1,256,256]{7,6,5,4,3,2,1,0:T(8,128)S(1)}, f32[1,3,1,1,1,1,256,256]{7,6,5,4,3,2,1,0:T(8,128)}, u32[]{:S(2)}) copy-start(f32[1,3,1,1,1,1,256,256]{7,6,5,4,3,2,1,0:T(8,128)} %param.20) | copy-start | bytes 2359300
  1270.9 243.7 %reduce-scatter.4.cloned.1.call-start = ((), (), s32[]{:S(2)}) async-start(), calls=%async_computation.7 | async-start | bytes 557056 | tf_op jit(solution)/shard_map/reduce_scatter | solution.py:44
  1439.5 310.9 %all-reduce.21.cloned.1.call-start = ((), (), s32[]{:S(2)}) async-start(), calls=%async_computation.8 | async-start | bytes 1048576 | tf_op jit(solution)/shard_map/psum | solution.py:11
  1515.3 33.9 %copy-start.11 = (f32[1,3,1,1,16,256]{5,4,3,2,1,0:T(8,128)S(1)}, f32[1,3,1,1,16,256]{5,4,3,2,1,0:T(8,128)}, u32[]{:S(2)}) copy-start(f32[1,3,1,1,16,256]{5,4,3,2,1,0:T(8,128)} %param.15) | copy-start | bytes 147460
  1583.8 1.8 copy-start.2
  1583.8 166.6 %copy-start.8 = (f32[1,3,1,1,1,1,256,256]{7,6,5,4,3,2,1,0:T(8,128)S(1)}, f32[1,3,1,1,1,1,256,256]{7,6,5,4,3,2,1,0:T(8,128)}, u32[]{:S(2)}) copy-start(f32[1,3,1,1,1,1,256,256]{7,6,5,4,3,2,1,0:T(8,128)} %param.19) | copy-start | bytes 2359300
  1583.8 244.0 %reduce-scatter.6.cloned.1.call-start = ((), (), s32[]{:S(2)}) async-start(), calls=%async_computation.9 | async-start | bytes 557056 | tf_op jit(solution)/shard_map/reduce_scatter | solution.py:44
  1752.9 311.2 %all-reduce.23.cloned.1.call-start = ((), (), s32[]{:S(2)}) async-start(), calls=%async_computation.10 | async-start | bytes 1048576 | tf_op jit(solution)/shard_map/psum | solution.py:11
  1897.0 244.6 %reduce-scatter.8.cloned.1.call-start = ((), (), s32[]{:S(2)}) async-start(), calls=%async_computation.11 | async-start | bytes 557056 | tf_op jit(solution)/shard_map/reduce_scatter | solution.py:44
  1897.1 1.0 copy-start.4
Sparse Core Ops, SparseCore 0:
  79.4 170.4 all-reduce.12
  253.1 142.7 all-reduce.24
  465.8 167.2 all-reduce.14
  636.3 142.7 all-reduce.26
  849.0 167.2 all-reduce.16
  1019.6 142.7 all-reduce.28
  1271.0 165.8 all-reduce.18
  1439.7 74.7 reduce-scatter.3
  1583.9 166.4 all-reduce.20
  1753.0 74.7 reduce-scatter.5
  1897.1 166.9 all-reduce.22
  2066.8 74.7 reduce-scatter.7
where the time goes:
time: 2190 us; the launch traced here: 2180 us
  waiting for transfers between devices  1640 us (75%)
  blocking collectives  479 us (22%)
  between operations  22.8 us (1%)
    psum x6, waiting for transfers between devices, broadcast(): return lax.psum(jnp.where(mine, x, jnp.zeros_like(x)), axis)  994 us
    unnamed x15, waiting for transfers between devices  425 us
    all_gather x8, blocking collectives, solve(): lax.all_gather(residual, 'col', axis=1, tiled=True)  278 us
    reduce_scatter x3, waiting for transfers between devices, solve(): lax.psum_scatter(partial_value, 'col', scatter_dimension=1, tiled=True)  223 us
    all_gather x6, blocking collectives, copy_out(): return spread(lax.all_gather(solution, 'col', axis=1, tiled=True))  198 us
  transfers between devices with their start and end apart: 12, of which 12 were waited for; matrix products, arithmetic and copies ran while one was open for 0% of the time, Pallas kernels for 0%

commit v1 on v0

--- a/solution.py
+++ b/solution.py
@@ -53,7 +53,17 @@
         )
 
     def copy_out(solution):
-        return spread(lax.all_gather(solution, "col", axis=1, tiled=True))
+        return spread(
+            jnp.concatenate(
+                lax.all_to_all(
+                    jnp.stack([solution for _ in range(lax.psum(1, axis_name="col"))], 0),
+                    split_axis=0,
+                    concat_axis=0,
+                    axis_name="col",
+                ),
+                1,
+            )
+        )
 
     def blocks(array, pair):
         return array[0, pair, :, 0, :, 0]

time: 2190 us -> 2090 us (0.954)
  blocking collectives: 479 us -> 332 us
  waiting for transfers between devices: 1640 us -> 1680 us
    all_gather x6 -> x0, blocking collectives: 198 us -> none  [copy_out(): return spread(lax.all_gather(solution, 'col', axis=1, tiled=True))]
    all_to_all x0 -> x3, blocking collectives: none -> 42.7 us  [copy_out(): lax.all_to_all(jnp.stack([solution for _ in range(lax.psum(1, axis_name='...]
    all_to_all x0 -> x3, waiting for transfers between devices: none -> 30.3 us  [copy_out(): lax.all_to_all(jnp.stack([solution for _ in range(lax.psum(1, axis_name='...]
  transfers between devices with their start and end apart: 12 -> 15, of which waited for: 12 -> 15; matrix products, arithmetic and copies ran while one was open for 0% -> 0% of each run, Pallas kernels for 0% -> 0%
where the time goes in v1:
time: 2090 us
  waiting for transfers between devices  1680 us (80%)
  blocking collectives  332 us (16%)
  between operations  22.7 us (1%)
  matrix products  21.7 us (1%)
    psum x6, waiting for transfers between devices, broadcast(): return lax.psum(jnp.where(mine, x, jnp.zeros_like(x)), axis)  1000 us
    unnamed x15, waiting for transfers between devices  427 us
    all_gather x8, blocking collectives, solve(): lax.all_gather(residual, 'col', axis=1, tiled=True)  285 us
    reduce_scatter x3, waiting for transfers between devices, solve(): lax.psum_scatter(partial_value, 'col', scatter_dimension=1, tiled=True)  225 us
    all_to_all x3, blocking collectives, copy_out(): lax.all_to_all(jnp.stack([solution for _ in range(lax.psum(1, axis_name='...  42.7 us
  transfers between devices with their start and end apart: 15, of which 15 were waited for; matrix products, arithmetic and copies ran while one was open for 0% of the time, Pallas kernels for 0%

profile of v1, /device:TPU:2, one launch (start us, length us, event | category | flops | bytes accessed | tf_op | source)
XLA Modules:
  0.0 2092.9 jit_solution(14755541993947713519)
XLA Ops:
  8.0 37.7 %all-gather = f32[1,1,1,1,256,512]{5,4,3,2,1,0:T(8,128)S(1)} all-gather(f32[1,1,1,1,16,512]{5,4,3,2,1,0:T(8,128)S(1)} %get-tuple-element.8), channel_id=2, replica_groups=mesh['layer'=2,'row'=16,'col'=16] {'col'}, dimensions={4}, use_global_device_ids=true | all-gather | bytes 557056 | tf_op jit(solution)/shard_map/all_gather | solution.py:51
  46.9 3.6 all-to-all-start
  50.6 11.3 all-to-all-done
  64.7 169.1 %all-reduce.13.cloned.1.call-done = f32[1,256,512]{2,1,0:T(8,128)} async-done(((f32[1,256,512]{2,1,0:T(8,128)}), f32[1,256,512]{2,1,0:T(8,128)}) %all-reduce.13.cloned.1.call-update) | async-done | bytes 524304 | tf_op jit(solution)/shard_map/psum | solution.py:11
  233.8 2.0 convolution_bitcast_fusion.1
  235.9 1.0 copy.24
  237.0 1.3 dynamic-slice
  239.0 140.8 %all-reduce.25.cloned.1.call-done = f32[1,256,512]{2,0,1:T(1,128)} async-done(((f32[1,256,512]{2,0,1:T(1,128)}), f32[1,256,512]{2,0,1:T(1,128)}) %all-reduce.25.cloned.1.call-update) | async-done | bytes 524304
  380.6 37.5 %all_gather.25 = f32[1,256,512]{2,0,1:T(1,128)S(1)} all-gather(f32[1,16,512]{2,0,1:T(1,128)S(1)} %fusion.84), channel_id=1, replica_groups=mesh['layer'=2,'row'=16,'col'=16] {'col'}, dimensions={1}, use_global_device_ids=true | all-gather | bytes 557056 | tf_op jit(solution)/shard_map/all_gather | solution.py:51
  418.6 14.0 all_to_all.30
  432.6 0.9 broadcast_select_fusion.4
  434.8 1.0 fusion.27
  435.8 165.8 %all-reduce.15.cloned.1.call-done = f32[1,256,512]{2,1,0:T(8,128)} async-done(((f32[1,256,512]{2,1,0:T(8,128)}), f32[1,256,512]{2,1,0:T(8,128)}) %all-reduce.15.cloned.1.call-update) | async-done | bytes 524304 | tf_op jit(solution)/shard_map/psum | solution.py:11
  601.7 2.0 fusion.3
  603.7 1.0 copy.26
  604.8 142.9 %all-reduce.27.cloned.1.call-done = f32[1,256,512]{2,0,1:T(1,128)} async-done(((f32[1,256,512]{2,0,1:T(1,128)}), f32[1,256,512]{2,0,1:T(1,128)}) %all-reduce.27.cloned.1.call-update) | async-done | bytes 524304
  748.5 35.7 %all_gather.26 = f32[1,256,512]{2,0,1:T(1,128)S(1)} all-gather(f32[1,16,512]{2,0,1:T(1,128)S(1)} %fusion.83), channel_id=1, replica_groups=mesh['layer'=2,'row'=16,'col'=16] {'col'}, dimensions={1}, use_global_device_ids=true | all-gather | bytes 557056 | tf_op jit(solution)/shard_map/all_gather | solution.py:51
  785.4 3.6 all-to-all-start.2
  791.0 9.4 all-to-all-done.2
  800.4 0.9 broadcast_select_fusion.3
  801.4 1.0 fusion.31
  802.4 1.0 convolution_add_fusion.5
  803.4 166.4 %all-reduce.17.cloned.1.call-done = f32[1,256,512]{2,1,0:T(8,128)} async-done(((f32[1,256,512]{2,1,0:T(8,128)}), f32[1,256,512]{2,1,0:T(8,128)}) %all-reduce.17.cloned.1.call-update) | async-done | bytes 524304 | tf_op jit(solution)/shard_map/psum | solution.py:11
  969.8 2.0 fusion.2
  971.8 1.0 copy.27
  972.9 142.8 %all-reduce.29.cloned.1.call-done = f32[1,256,512]{2,0,1:T(1,128)} async-done(((f32[1,256,512]{2,0,1:T(1,128)}), f32[1,256,512]{2,0,1:T(1,128)}) %all-reduce.29.cloned.1.call-update) | async-done | bytes 524304
  1116.5 3.5 psum.52
  1120.1 35.3 %all_gather.27 = f32[1,256,512]{2,0,1:T(1,128)S(1)} all-gather(f32[1,16,512]{2,0,1:T(1,128)S(1)} %reshape_subtract_fusion), channel_id=1, replica_groups=mesh['layer'=2,'row'=16,'col'=16] {'col'}, dimensions={1}, use_global_device_ids=true | all-gather | bytes 557056 | tf_op jit(solution)/shard_map/all_gather | solution.py:51
  1155.8 34.6 %all-gather.1 = f32[256,512]{1,0:T(8,128)S(1)} all-gather(f32[16,512]{1,0:T(8,128)S(1)} %convolution_bitcast_fusion.3), channel_id=3, replica_groups=mesh['layer'=2,'row'=16,'col'=16] {'col'}, dimensions={0}, use_global_device_ids=true | all-gather | bytes 557056 | tf_op jit(solution)/shard_map/all_gather | solution.py:51
  1191.4 14.6 all_to_all.31
  1207.5 168.1 %all-reduce.19.cloned.1.call-done = f32[1,256,512]{2,1,0:T(8,128)} async-done(((f32[1,256,512]{2,1,0:T(8,128)}), f32[1,256,512]{2,1,0:T(8,128)}) %all-reduce.19.cloned.1.call-update) | async-done | bytes 524304 | tf_op jit(solution)/shard_map/psum | solution.py:11
  1375.6 2.5 convolution_bitcast_fusion
  1378.2 75.0 %reduce-scatter.4.cloned.1.call-done = f32[1,16,512]{2,1,0:T(8,128)} async-done(((f32[1,256,512]{2,1,0:T(8,128)}), f32[1,16,512]{2,1,0:T(8,128)}) %reduce-scatter.4.cloned.1.call-update) | async-done | bytes 32784 | tf_op jit(solution)/shard_map/reduce_scatter | solution.py:44
  1454.0 35.9 %all_gather.29 = f32[1,256,512]{2,1,0:T(8,128)S(1)} all-gather(f32[1,16,512]{2,1,0:T(8,128)S(1)} %bitcast_subtract_fusion.1), channel_id=1, replica_groups=mesh['layer'=2,'row'=16,'col'=16] {'col'}, dimensions={1}, use_global_device_ids=true | all-gather | bytes 557056 | tf_op jit(solution)/shard_map/all_gather | solution.py:51
  1490.4 14.0 all_to_all.32
  1504.4 0.9 broadcast_select_fusion.1
  1507.4 166.2 %all-reduce.21.cloned.1.call-done = f32[1,256,512]{2,1,0:T(8,128)} async-done(((f32[1,256,512]{2,1,0:T(8,128)}), f32[1,256,512]{2,1,0:T(8,128)}) %all-reduce.21.cloned.1.call-update) | async-done | bytes 524304 | tf_op jit(solution)/shard_map/psum | solution.py:11
  1673.6 2.5 fusion.1
  1676.1 74.9 %reduce-scatter.6.cloned.1.call-done = f32[1,16,512]{2,1,0:T(8,128)} async-done(((f32[1,256,512]{2,1,0:T(8,128)}), f32[1,16,512]{2,1,0:T(8,128)}) %reduce-scatter.6.cloned.1.call-update) | async-done | bytes 32784 | tf_op jit(solution)/shard_map/reduce_scatter | solution.py:44
  1751.8 34.9 %all_gather.30 = f32[1,256,512]{2,1,0:T(8,128)S(1)} all-gather(f32[1,16,512]{2,1,0:T(8,128)S(1)} %bitcast_subtract_fusion), channel_id=1, replica_groups=mesh['layer'=2,'row'=16,'col'=16] {'col'}, dimensions={1}, use_global_device_ids=true | all-gather | bytes 557056 | tf_op jit(solution)/shard_map/all_gather | solution.py:51
  1787.1 0.9 stack.27
  1788.0 3.6 all-to-all-start.5
  1793.4 9.5 all-to-all-done.5
  1803.0 0.9 broadcast_select_fusion
  1805.6 167.4 %all-reduce.23.cloned.1.call-done = f32[1,256,512]{2,1,0:T(8,128)} async-done(((f32[1,256,512]{2,1,0:T(8,128)}), f32[1,256,512]{2,1,0:T(8,128)}) %all-reduce.23.cloned.1.call-update) | async-done | bytes 524304 | tf_op jit(solution)/shard_map/psum | solution.py:11
  1973.0 2.5 fusion
  1975.5 75.0 %reduce-scatter.8.cloned.1.call-done = f32[1,16,512]{2,1,0:T(8,128)} async-done(((f32[1,256,512]{2,1,0:T(8,128)}), f32[1,16,512]{2,1,0:T(8,128)}) %reduce-scatter.8.cloned.1.call-update) | async-done | bytes 32784 | tf_op jit(solution)/shard_map/reduce_scatter | solution.py:44
  2051.2 33.8 %all_gather.31 = f32[1,256,512]{2,1,0:T(8,128)S(1)} all-gather(f32[1,16,512]{2,1,0:T(8,128)S(1)} %bitcast_subtract_fusion.2), channel_id=1, replica_groups=mesh['layer'=2,'row'=16,'col'=16] {'col'}, dimensions={1}, use_global_device_ids=true | all-gather | bytes 557056 | tf_op jit(solution)/shard_map/all_gather | solution.py:51
  (82 shorter events, 17.8 us)
Async XLA Ops:
  7.2 1148.2 %copy-start = (f32[1,1,16,256]{3,2,1,0:T(8,128)S(1)}, f32[1,1,16,256]{3,2,1,0:T(8,128)}, u32[]{:S(2)}) copy-start(f32[1,1,16,256]{3,2,1,0:T(8,128)} %param.14) | copy-start | bytes 49156
  8.0 37.7 %copy-start.10 = (f32[1,3,1,1,16,256]{5,4,3,2,1,0:T(8,128)S(1)}, f32[1,3,1,1,16,256]{5,4,3,2,1,0:T(8,128)}, u32[]{:S(2)}) copy-start(f32[1,3,1,1,16,256]{5,4,3,2,1,0:T(8,128)} %param.13) | copy-start | bytes 147460
  46.9 15.0 all-to-all-start
  50.5 183.3 %all-reduce.13.cloned.1.call-start = ((), (), s32[]{:S(2)}) async-start(), calls=%async_computation.9 | async-start | bytes 1048576 | tf_op jit(solution)/shard_map/psum | solution.py:11
  50.6 183.3 %copy-start.6 = (f32[1,3,1,1,1,1,256,256]{7,6,5,4,3,2,1,0:T(8,128)S(1)}, f32[1,3,1,1,1,1,256,256]{7,6,5,4,3,2,1,0:T(8,128)}, u32[]{:S(2)}) copy-start(f32[1,3,1,1,1,1,256,256]{7,6,5,4,3,2,1,0:T(8,128)} %param.17) | copy-start | bytes 2359300
  62.7 0.7 copy-start.13
  62.7 317.1 %all-reduce.25.cloned.1.call-start = ((), (), s32[]{:S(2)}) async-start(), calls=%async_computation.18 | async-start | bytes 1048576
  236.9 364.7 %all-reduce.15.cloned.1.call-start = ((), (), s32[]{:S(2)}) async-start(), calls=%async_computation.10 | async-start | bytes 1048576 | tf_op jit(solution)/shard_map/psum | solution.py:11
  433.5 1.3 copy-start.1
  433.5 314.1 %all-reduce.27.cloned.1.call-start = ((), (), s32[]{:S(2)}) async-start(), calls=%async_computation.19 | async-start | bytes 1048576
  785.4 15.0 all-to-all-start.2
  789.0 180.7 %all-reduce.17.cloned.1.call-start = ((), (), s32[]{:S(2)}) async-start(), calls=%async_computation.11 | async-start | bytes 1048576 | tf_op jit(solution)/shard_map/psum | solution.py:11
  791.0 10.4 copy-start.7
  801.3 314.5 %all-reduce.29.cloned.1.call-start = ((), (), s32[]{:S(2)}) async-start(), calls=%async_computation.20 | async-start | bytes 1048576
  801.3 1.0 copy-start.3
  972.9 402.7 %all-reduce.19.cloned.1.call-start = ((), (), s32[]{:S(2)}) async-start(), calls=%async_computation.12 | async-start | bytes 1048576 | tf_op jit(solution)/shard_map/psum | solution.py:11
  1116.5 3.5 copy-start.12
  1155.8 34.6 %copy-start.14 = (f32[1,1,16,256]{3,2,1,0:T(8,128)S(1)}, f32[1,1,16,256]{3,2,1,0:T(8,128)}, u32[]{:S(2)}) copy-start(f32[1,1,16,256]{3,2,1,0:T(8,128)} %param.16) | copy-start | bytes 49156
  1190.7 0.6 copy-start.9
  1206.0 169.6 %copy-start.5 = (f32[1,3,1,1,1,1,256,256]{7,6,5,4,3,2,1,0:T(8,128)S(1)}, f32[1,3,1,1,1,1,256,256]{7,6,5,4,3,2,1,0:T(8,128)}, u32[]{:S(2)}) copy-start(f32[1,3,1,1,1,1,256,256]{7,6,5,4,3,2,1,0:T(8,128)} %param.20) | copy-start | bytes 2359300
  1206.9 246.4 %reduce-scatter.4.cloned.1.call-start = ((), (), s32[]{:S(2)}) async-start(), calls=%async_computation.13 | async-start | bytes 557056 | tf_op jit(solution)/shard_map/reduce_scatter | solution.py:44
  1378.1 295.5 %all-reduce.21.cloned.1.call-start = ((), (), s32[]{:S(2)}) async-start(), calls=%async_computation.14 | async-start | bytes 1048576 | tf_op jit(solution)/shard_map/psum | solution.py:11
  1454.0 35.9 %copy-start.11 = (f32[1,3,1,1,16,256]{5,4,3,2,1,0:T(8,128)S(1)}, f32[1,3,1,1,16,256]{5,4,3,2,1,0:T(8,128)}, u32[]{:S(2)}) copy-start(f32[1,3,1,1,16,256]{5,4,3,2,1,0:T(8,128)} %param.15) | copy-start | bytes 147460
  1505.3 1.4 copy-start.2
  1505.3 168.3 %copy-start.8 = (f32[1,3,1,1,1,1,256,256]{7,6,5,4,3,2,1,0:T(8,128)S(1)}, f32[1,3,1,1,1,1,256,256]{7,6,5,4,3,2,1,0:T(8,128)}, u32[]{:S(2)}) copy-start(f32[1,3,1,1,1,1,256,256]{7,6,5,4,3,2,1,0:T(8,128)} %param.19) | copy-start | bytes 2359300
  1505.3 245.8 %reduce-scatter.6.cloned.1.call-start = ((), (), s32[]{:S(2)}) async-start(), calls=%async_computation.15 | async-start | bytes 557056 | tf_op jit(solution)/shard_map/reduce_scatter | solution.py:44
  1788.0 15.0 all-to-all-start.5
  1791.6 181.4 %all-reduce.23.cloned.1.call-start = ((), (), s32[]{:S(2)}) async-start(), calls=%async_computation.16 | async-start | bytes 1048576 | tf_op jit(solution)/shard_map/psum | solution.py:11
  1803.8 246.6 %reduce-scatter.8.cloned.1.call-start = ((), (), s32[]{:S(2)}) async-start(), calls=%async_computation.17 | async-start | bytes 557056 | tf_op jit(solution)/shard_map/reduce_scatter | solution.py:44
  1803.9 1.0 copy-start.4
Sparse Core Ops, SparseCore 0:
  62.9 170.9 all-reduce.12
  237.0 142.7 all-reduce.24
  433.6 167.9 all-reduce.14
  604.9 142.7 all-reduce.26
  801.4 168.3 all-reduce.16
  973.0 142.7 all-reduce.28
  1207.0 168.5 all-reduce.18
  1378.4 74.7 reduce-scatter.3
  1505.4 168.1 all-reduce.20
  1676.2 74.7 reduce-scatter.5
  1804.0 169.0 all-reduce.22
  1975.7 74.7 reduce-scatter.7
